TPU v7x, 512 devices: a whole 4x8x8 slice. The times are simulated.
512 devices in a mesh: section: 64 (over z, y_hi, core), tensor: 8 (over x, y_lo).
Axes of the slice: x: 4, y: 8 (y_hi: 4, y_lo: 2; y = y_hi * 2 + y_lo), z: 8, core: 2. Of those that a mesh axis runs over, the one named last changes fastest.
Arguments:
- grad_in: bfloat16 [64, 256, 6144], P('section', None, 'tensor'), may hold values from -6 to 6
- loss_grad: bfloat16 [256, 6144], P(None, 'tensor'), may hold values from -6 to 6
- queries: bfloat16 [64, 2, 256, 6144], P('section', None, None, 'tensor'), may hold values from -32 to 32
- attn_keys: bfloat16 [64, 2, 256, 6144], P('section', None, None, 'tensor'), may hold values from -32 to 32
- stored_input: bfloat16 [64, 2, 256, 6144], P('section', None, 'tensor'), may hold values from -6 to 6
- block_scales: bfloat16 [64, 2, 256, 48], P('section', None, 'tensor'), may hold values from 0.25 to 4
Outputs:
- grad_next: bfloat16 [64, 256, 6144], P('section', None, 'tensor')
- query_grad: bfloat16 [64, 2, 256, 6144], P('section', None, None, 'tensor')
- key_grad: bfloat16 [64, 2, 256, 6144], P('section', None, None, 'tensor')
All inputs are finite; a program needn't handle non-finite values.
Results may differ from a plain program's by a relative error of at most 0.0063.
Values may be sent and summed in bfloat16 or wider, within the bound.
A program may use at most 64 MiB of HBM per device.

v0:
```python
import math

import jax
import jax.numpy as jnp
from jax import lax
from jax.sharding import PartitionSpec as P

HD = 128


def passed_along(value, axis, steps):
    count = lax.axis_size(axis)
    leading, last = (max(0, -steps), min(count, count - steps))
    return lax.ppermute(value, axis, [(source, source + steps) for source in range(leading, last)])


def to_heads(flat):
    tokens, width = flat.shape
    return flat.reshape(tokens, width // HD, HD).transpose(1, 0, 2)


def from_heads(split):
    heads, tokens, depth = split.shape
    return split.transpose(1, 0, 2).reshape(tokens, heads * depth)


def attention_weights(query_heads, key_heads):
    tokens = query_heads.shape[1]
    scores = jnp.einsum(
        "htd,hjd->htj", query_heads, key_heads, preferred_element_type=jnp.float32
    ) * (1.0 / math.sqrt(HD))
    causal = lax.broadcasted_iota(jnp.int32, (tokens, tokens), 0) >= lax.broadcasted_iota(
        jnp.int32, (tokens, tokens), 1
    )
    scores = jnp.where(causal[None], scores, -1e30)
    scores = scores - jnp.max(scores, axis=-1, keepdims=True)
    expon = jnp.exp(scores)
    return expon / jnp.sum(expon, axis=-1, keepdims=True)


def value_grad(weights, upstream, upstream_heads):
    rounded = weights.astype(jnp.bfloat16)
    carried = jnp.einsum(
        "htj,htd->hjd", rounded, upstream_heads, preferred_element_type=jnp.float32
    )
    return (upstream.astype(jnp.float32) + from_heads(carried)).astype(jnp.bfloat16)


def score_grads(weights, upstream_heads, input_heads, query_heads, key_heads):
    product = jnp.einsum(
        "htd,hjd->htj", upstream_heads, input_heads, preferred_element_type=jnp.float32
    )
    centre = jnp.sum(weights * product, axis=-1, keepdims=True)
    score_diff = (weights * (product - centre)).astype(jnp.bfloat16)
    scaling = 1.0 / math.sqrt(HD)
    query_out = (
        jnp.einsum("htj,hjd->htd", score_diff, key_heads, preferred_element_type=jnp.float32)
        * scaling
    ).astype(jnp.bfloat16)
    key_out = (
        jnp.einsum("htj,htd->hjd", score_diff, query_heads, preferred_element_type=jnp.float32)
        * scaling
    ).astype(jnp.bfloat16)
    return (from_heads(query_out), from_heads(key_out))


def dequantize(values, scales):
    value_heads = to_heads(values).astype(jnp.float32)
    scale_heads = scales.astype(jnp.float32).T[:, :, None]
    return (value_heads * scale_heads).astype(jnp.bfloat16)


def local(grad_in, loss_grad, queries, attn_keys, stored_input, block_scales):
    grad_first = grad_in[0]
    query_pair = queries[0]
    key_pair = attn_keys[0]
    is_last = lax.axis_index("section") == lax.axis_size("section") - 1
    query_first_heads = to_heads(query_pair[0])
    key_first_heads = to_heads(key_pair[0])
    grad_first_heads = to_heads(grad_first)
    weights_first = attention_weights(query_first_heads, key_first_heads)
    input_first = value_grad(weights_first, grad_first, grad_first_heads)
    received = passed_along(input_first, "section", -1)
    grad_second = jnp.where(is_last, loss_grad, received)
    grad_second_heads = to_heads(grad_second)
    query_second_heads = to_heads(query_pair[1])
    key_second_heads = to_heads(key_pair[1])
    weights_second = attention_weights(query_second_heads, key_second_heads)
    input_second = value_grad(weights_second, grad_second, grad_second_heads)
    columns, column_scales = (
        lax.all_to_all(stored_input[0], "tensor", split_axis=2, concat_axis=1, tiled=True),
        lax.all_to_all(block_scales[0], "tensor", split_axis=2, concat_axis=1, tiled=True),
    )
    inputs_first = dequantize(columns[0], column_scales[0])
    inputs_second = dequantize(columns[1], column_scales[1])
    query_first, key_first = score_grads(
        weights_first, grad_first_heads, inputs_first, query_first_heads, key_first_heads
    )
    query_second, key_second = score_grads(
        weights_second, grad_second_heads, inputs_second, query_second_heads, key_second_heads
    )
    grad_next = passed_along(input_second, "section", -1)
    query_grad = jnp.stack([query_first, query_second])
    key_grad = jnp.stack([key_first, key_second])
    return (grad_next[None], query_grad[None], key_grad[None])


def solution(mesh):
    return jax.shard_map(
        local,
        mesh=mesh,
        in_specs=(
            P("section", None, "tensor"),
            P(None, "tensor"),
            P("section", None, None, "tensor"),
            P("section", None, None, "tensor"),
            P("section", None, "tensor", None),
            P("section", None, "tensor", None),
        ),
        out_specs=(
            P("section", None, "tensor"),
            P("section", None, None, "tensor"),
            P("section", None, None, "tensor"),
        ),
        check_vma=False,
    )
```

profile of v0, /device:TPU:249, one launch (start us, length us, event | category | flops | bytes accessed | tf_op | source)
XLA Modules:
  0.0 87.2 jit_solution(11047999192089381704)
XLA Ops:
  0.6 0.6 iota_compare_fusion
  1.3 2.0 %fusion.51 = (bf16[1,1,256,768]{3,2,1,0:T(8,128)(2,1)}, bf16[1,1,256,768]{3,2,1,0:T(8,128)(2,1)S(1)}) fusion(bf16[1,2,256,768]{3,2,1,0:T(8,128)(2,1)} %param.8), kind=kLoop, calls=%fused_computation.60 | loop fusion | bytes 1572864 | tf_op jit(solution)/shard_map/slice | solution.py:86
  3.3 0.2 copy.158
  3.4 0.2 copy.104
  3.7 0.8 fusion.52
  4.5 0.2 copy.159
  4.7 0.2 copy.106
  4.9 0.2 copy.102
  5.1 1.6 %fusion.53 = (f32[6,256]{1,0:T(8,128)S(1)}, f32[6,256,256]{1,2,0:T(8,128)S(1)}) fusion(pred[256,256]{0,1:T(8,128)(4,1)} %iota_compare_fusion, bf16[256,6,128]{2,0,1:T(8,128)(2,1)S(1)} %copy.106, bf16[256,6,128]{2,0,1:T(8,128)(2,1)S(1)} %copy.104), kind=kOutput, calls=%fused_computation.62 | convolution fusion | flops 102236416 | bytes 2430976 | tf_op jit(solution)/shard_map/sub | solution.py:36
  6.7 0.4 fusion.19
  7.1 0.7 copy-done.7
  7.8 0.8 fusion.16
  8.7 2.6 %collective-permute-start = (bf16[256,768]{0,1:T(8,128)(2,1)}, bf16[256,768]{0,1:T(8,128)(2,1)}, u32[]{:S(2)}, u32[]{:S(2)}) collective-permute-start(bf16[256,768]{0,1:T(8,128)(2,1)} %fusion.16), channel_id=1, source_target_pairs={{8,0},{16,8},{24,16},{32,24},{40,32},{48,40},{56,48},{64,56},{72,6... | collective-permute-start | bytes 1179656 | tf_op jit(solution)/shard_map/ppermute | solution.py:14
  11.2 0.1 copy.117
  11.4 0.7 reshape.66
  12.1 5.2 %all-to-all-start.1 = ((bf16[8,2,192]{2,1,0:T(2,128)(2,1)}), bf16[8,2,192]{2,1,0:T(2,128)(2,1)S(1)}, u32[]{:S(2)}, u32[]{:S(2)}) async-start(bf16[8,2,192]{2,1,0:T(2,128)(2,1)} %reshape.66), calls=%async_computation.1 | async-start | bytes 16384 | tf_op jit(solution)/shard_map/all_to_all | solution.py:92
  17.3 5.1 %copy.115 = bf16[1,2,32,6144]{2,1,3,0:T(2,128)(2,1)} copy(bf16[1,2,32,6144]{3,2,1,0:T(8,128)(2,1)S(1)} %copy-done.14) | data formatting | bytes 1572864 | tf_op args[4]
  22.4 4.7 %bitcast_bitcast_fusion = bf16[6144,2,32]{2,1,0:T(2,128)(2,1)S(1)} fusion(bf16[1,2,32,6144]{2,1,3,0:T(2,128)(2,1)} %copy.115), kind=kLoop, calls=%fused_computation.64 | loop fusion | bytes 1572864
  27.1 1.9 %copy.109 = bf16[256,768]{0,1:T(8,128)(2,1)} copy(bf16[256,768]{1,0:T(8,128)(2,1)} %param.7) | data formatting | bytes 786432 | tf_op args[1]
  29.0 1.9 %copy.160 = bf16[1,1,256,768]{2,3,1,0:T(8,128)(2,1)} copy(bf16[1,1,256,768]{3,2,1,0:T(8,128)(2,1)} %get-tuple-element.14) | data formatting | bytes 786432
  30.9 1.9 %copy.111 = bf16[256,6,128]{2,0,1:T(8,128)(2,1)} copy(bf16[256,6,128]{0,2,1:T(8,128)(2,1)} %bitcast.150) | data formatting | bytes 786432 | tf_op jit(solution)/shard_map/reshape;squeeze | solution.py:19
  32.8 1.9 %copy.161 = bf16[1,1,256,768]{2,3,1,0:T(8,128)(2,1)} copy(bf16[1,1,256,768]{3,2,1,0:T(8,128)(2,1)} %get-tuple-element.16) | data formatting | bytes 786432
  34.7 1.9 %copy.113 = bf16[256,6,128]{2,0,1:T(8,128)(2,1)} copy(bf16[256,6,128]{0,2,1:T(8,128)(2,1)} %bitcast.152) | data formatting | bytes 786432 | tf_op jit(solution)/shard_map/reshape;squeeze | solution.py:19
  36.7 3.7 %reshape.64 = bf16[8,2,24576]{2,1,0:T(2,128)(2,1)} reshape(bf16[6144,2,32]{2,1,0:T(2,128)(2,1)S(1)} %bitcast_bitcast_fusion) | data formatting | bytes 1572864
  40.3 5.3 %all-to-all-start = ((bf16[8,2,24576]{2,1,0:T(2,128)(2,1)}), bf16[8,2,24576]{2,1,0:T(2,128)(2,1)}, u32[]{:S(2)}, u32[]{:S(2)}) async-start(bf16[8,2,24576]{2,1,0:T(2,128)(2,1)} %reshape.64), calls=%async_computation | async-start | bytes 1572864 | tf_op jit(solution)/shard_map/all_to_all | solution.py:91
  45.7 0.6 fusion.58
  46.3 0.3 copy-done.6
  46.6 1.3 %broadcast_select_fusion = bf16[256,768]{0,1:T(8,128)(2,1)S(1)} fusion(bf16[256,768]{0,1:T(8,128)(2,1)S(1)} %copy-done.6, bf16[256,768]{0,1:T(8,128)(2,1)} %collective-permute-done, pred[]{:T(512)S(6)} %eq.3), kind=kLoop, calls=%fused_computation.49 | loop fusion | flops 196608 | bytes 1179649 | tf_op jit(solution)/shard_map/jit(_where)/select_n | solution.py:84
  47.9 0.4 fusion.17
  48.3 0.3 copy-done.11
  48.7 0.1 fusion.15
  48.8 4.6 %collective-permute-start.1 = (bf16[256,768]{0,1:T(8,128)(2,1)S(1)}, bf16[256,768]{0,1:T(8,128)(2,1)S(1)}, u32[]{:S(2)}, u32[]{:S(2)}) collective-permute-start(bf16[256,768]{0,1:T(8,128)(2,1)S(1)} %fusion.15), channel_id=1, source_target_pairs={{8,0},{16,8},{24,16},{32,24},{40,32},{48,40},{56,48},{64,56},{72,6... | collective-permute-start | bytes 1179656 | tf_op jit(solution)/shard_map/ppermute | solution.py:14
  53.4 0.1 reshape.67
  53.5 0.1 reshape.63
  53.6 0.8 copy.124
  54.4 0.8 copy.119
  55.2 12.1 %collective-permute-done.1 = bf16[256,768]{0,1:T(8,128)(2,1)S(1)} collective-permute-done((bf16[256,768]{0,1:T(8,128)(2,1)S(1)}, bf16[256,768]{0,1:T(8,128)(2,1)S(1)}, u32[]{:S(2)}, u32[]{:S(2)}) %collective-permute-start.1) | collective-permute-done | bytes 393248 | tf_op jit(solution)/shard_map/ppermute | solution.py:14
  67.3 0.9 %copy.137 = bf16[1,256,768]{2,1,0:T(8,128)(2,1)} copy(bf16[1,256,768]{1,2,0:T(8,128)(2,1)S(1)} %bitcast.163) | data formatting | bytes 786432
  68.2 3.2 %reshape.65 = bf16[6144,2,32]{2,1,0:T(2,128)(2,1)S(1)} reshape(bf16[8,2,24576]{2,1,0:T(2,128)(2,1)} %all-to-all-done) | data formatting | bytes 1572864
  71.4 4.9 %copy.116 = bf16[2,32,8,768]{3,1,2,0:T(8,128)(2,1)} copy(bf16[2,32,8,768]{1,0,3,2:T(2,128)(2,1)S(1)} %bitcast.145) | data formatting | bytes 1572864 | tf_op jit(solution)/shard_map/all_to_all | solution.py:91
  76.4 1.3 %slice_convert_fusion.1 = (f32[1,8,32,768]{3,2,1,0:T(8,128)S(1)}, f32[1,8,32,768]{3,2,1,0:T(8,128)S(1)}) fusion(bf16[2,8,32,768]{3,2,1,0:T(8,128)(2,1)} %bitcast.154), kind=kLoop, calls=%fused_computation.40 | loop fusion | flops 393216 | bytes 2359296 | tf_op jit(solution)/shard_map/convert_element_type | solution.py:68
  77.7 0.1 reshape.62
  77.8 0.3 fusion.13
  78.2 0.5 copy-done.12
  78.7 0.6 copy-done.10
  79.3 0.4 multiply_reduce_fusion
  79.7 0.3 multiply_convert_fusion
  80.0 0.7 copy-done.2
  80.6 0.4 fusion.10
  81.0 0.2 copy.136
  81.2 0.3 fusion.12
  81.5 0.2 copy.130
  81.7 0.1 reshape.60
  81.8 0.6 copy-done.15
  82.4 0.3 fusion.14
  82.8 1.1 %copy-done.8 = f32[6,256,256]{1,2,0:T(8,128)S(1)} copy-done((f32[6,256,256]{1,2,0:T(8,128)S(1)}, f32[6,256,256]{1,2,0:T(8,128)}, u32[]{:S(2)}) %copy-start.8) | copy-done | bytes 1572888
  83.9 0.4 fusion.4
  84.2 0.3 fusion.6
  84.5 0.4 fusion.9
  84.9 0.2 copy.135
  85.1 0.4 copy-done.1
  85.5 0.3 fusion.11
  85.8 0.2 copy.129
  86.0 1.3 %maximum_bitcast_fusion = (bf16[1,2,256,768]{3,2,1,0:T(8,128)(2,1)}, bf16[1,2,256,768]{3,2,1,0:T(8,128)(2,1)}) fusion(bf16[1,256,768]{2,1,0:T(8,128)(2,1)S(1)} %copy.130, bf16[1,256,768]{2,1,0:T(8,128)(2,1)S(1)} %copy.129, bf16[1,256,768]{2,1,0:T(8,128)(2,1)S(1)} %copy.136, bf16[1,256,768]{2,1,0:T(8,128)(2,1)S(1)} %copy.135), kind=kLoop, calls=%fused_computation.27 | loop fusion | flops 786432 | bytes 3145728 | tf_op jit(solution)/shard_map/broadcast_in_dim | solution.py:105
  (46 shorter events, 0.2 us)
Async XLA Ops:
  1.3 2.4 %copy-start.13 = (bf16[1,2,256,768]{3,2,1,0:T(8,128)(2,1)S(1)}, bf16[1,2,256,768]{3,2,1,0:T(8,128)(2,1)}, u32[]{:S(2)}) copy-start(bf16[1,2,256,768]{3,2,1,0:T(8,128)(2,1)} %param.9) | copy-start | bytes 2359300
  3.7 1.2 %copy-start.17 = (bf16[1,256,768]{2,1,0:T(8,128)(2,1)S(1)}, bf16[1,256,768]{2,1,0:T(8,128)(2,1)}, u32[]{:S(2)}) copy-start(bf16[1,256,768]{2,1,0:T(8,128)(2,1)} %param.6) | copy-start | bytes 1179652
  4.7 2.0 %copy-start = (bf16[1,1,256,768]{2,3,1,0:T(8,128)(2,1)}, bf16[1,1,256,768]{2,3,1,0:T(8,128)(2,1)S(1)}, u32[]{:S(2)}) copy-start(bf16[1,1,256,768]{2,3,1,0:T(8,128)(2,1)S(1)} %copy.159) | copy-start | bytes 1179652
  5.1 2.0 %copy-start.4 = (bf16[1,256,768]{1,2,0:T(8,128)(2,1)}, bf16[1,256,768]{1,2,0:T(8,128)(2,1)S(1)}, u32[]{:S(2)}) copy-start(bf16[1,256,768]{1,2,0:T(8,128)(2,1)S(1)} %copy.102) | copy-start | bytes 1179652
  6.7 1.2 %copy-start.7 = (f32[6,256,256]{1,2,0:T(8,128)}, f32[6,256,256]{1,2,0:T(8,128)S(1)}, u32[]{:S(2)}) copy-start(f32[6,256,256]{1,2,0:T(8,128)S(1)} %get-tuple-element.21) | copy-start | bytes 4718596
  7.8 3.4 %copy-start.21 = (bf16[1,2,32,48]{3,2,1,0:T(8,128)(2,1)S(1)}, bf16[1,2,32,48]{3,2,1,0:T(8,128)(2,1)}, u32[]{:S(2)}) copy-start(bf16[1,2,32,48]{3,2,1,0:T(8,128)(2,1)} %param.11) | copy-start | bytes 18436
  7.8 9.4 %copy-start.14 = (bf16[1,2,32,6144]{3,2,1,0:T(8,128)(2,1)S(1)}, bf16[1,2,32,6144]{3,2,1,0:T(8,128)(2,1)}, u32[]{:S(2)}) copy-start(bf16[1,2,32,6144]{3,2,1,0:T(8,128)(2,1)} %param.10) | copy-start | bytes 2359300
  8.7 37.7 %collective-permute-start = (bf16[256,768]{0,1:T(8,128)(2,1)}, bf16[256,768]{0,1:T(8,128)(2,1)}, u32[]{:S(2)}, u32[]{:S(2)}) collective-permute-start(bf16[256,768]{0,1:T(8,128)(2,1)} %fusion.16), channel_id=1, source_target_pairs={{8,0},{16,8},{24,16},{32,24},{40,32},{48,40},{56,48},{64,56},{72,6... | collective-permute-start | bytes 1179656 | tf_op jit(solution)/shard_map/ppermute | solution.py:14
  12.1 28.3 %all-to-all-start.1 = ((bf16[8,2,192]{2,1,0:T(2,128)(2,1)}), bf16[8,2,192]{2,1,0:T(2,128)(2,1)S(1)}, u32[]{:S(2)}, u32[]{:S(2)}) async-start(bf16[8,2,192]{2,1,0:T(2,128)(2,1)} %reshape.66), calls=%async_computation.1 | async-start | bytes 16384 | tf_op jit(solution)/shard_map/all_to_all | solution.py:92
  40.3 5.3 %copy-start.18 = (bf16[256,6,128]{2,0,1:T(8,128)(2,1)S(1)}, bf16[256,6,128]{2,0,1:T(8,128)(2,1)}, u32[]{:S(2)}) copy-start(bf16[256,6,128]{2,0,1:T(8,128)(2,1)} %copy.111) | copy-start | bytes 1179652
  40.3 5.3 %copy-start.19 = (bf16[256,6,128]{2,0,1:T(8,128)(2,1)S(1)}, bf16[256,6,128]{2,0,1:T(8,128)(2,1)}, u32[]{:S(2)}) copy-start(bf16[256,6,128]{2,0,1:T(8,128)(2,1)} %copy.113) | copy-start | bytes 1179652
  40.3 5.3 %copy-start.20 = (pred[256,256]{0,1:T(8,128)(4,1)S(1)}, pred[256,256]{0,1:T(8,128)(4,1)}, u32[]{:S(2)}) copy-start(pred[256,256]{0,1:T(8,128)(4,1)} %iota_compare_fusion) | copy-start | bytes 196612
  40.3 27.9 %all-to-all-start = ((bf16[8,2,24576]{2,1,0:T(2,128)(2,1)}), bf16[8,2,24576]{2,1,0:T(2,128)(2,1)}, u32[]{:S(2)}, u32[]{:S(2)}) async-start(bf16[8,2,24576]{2,1,0:T(2,128)(2,1)} %reshape.64), calls=%async_computation | async-start | bytes 1572864 | tf_op jit(solution)/shard_map/all_to_all | solution.py:91
  45.6 1.0 %copy-start.6 = (bf16[256,768]{0,1:T(8,128)(2,1)S(1)}, bf16[256,768]{0,1:T(8,128)(2,1)}, u32[]{:S(2)}) copy-start(bf16[256,768]{0,1:T(8,128)(2,1)} %copy.109) | copy-start | bytes 1179652
  46.3 2.0 %copy-start.9 = (f32[6,256,256]{1,2,0:T(8,128)}, f32[6,256,256]{1,2,0:T(8,128)S(1)}, u32[]{:S(2)}) copy-start(f32[6,256,256]{1,2,0:T(8,128)S(1)} %get-tuple-element.23) | copy-start | bytes 4718596
  46.3 2.0 %copy-start.22 = (f32[6,256]{1,0:T(8,128)}, f32[6,256]{1,0:T(8,128)S(1)}, u32[]{:S(2)}) copy-start(f32[6,256]{1,0:T(8,128)S(1)} %get-tuple-element.22) | copy-start | bytes 18436
  47.9 0.8 copy-start.11
  48.8 18.5 %collective-permute-start.1 = (bf16[256,768]{0,1:T(8,128)(2,1)S(1)}, bf16[256,768]{0,1:T(8,128)(2,1)S(1)}, u32[]{:S(2)}, u32[]{:S(2)}) collective-permute-start(bf16[256,768]{0,1:T(8,128)(2,1)S(1)} %fusion.15), channel_id=1, source_target_pairs={{8,0},{16,8},{24,16},{32,24},{40,32},{48,40},{56,48},{64,56},{72,6... | collective-permute-start | bytes 1179656 | tf_op jit(solution)/shard_map/ppermute | solution.py:14
  76.4 1.5 %copy-start.16 = (f32[6,256]{0,1:T(8,128)S(1)}, f32[6,256]{0,1:T(8,128)}, u32[]{:S(2)}) copy-start(f32[6,256]{0,1:T(8,128)} %copy.124) | copy-start | bytes 18436
  77.7 1.0 %copy-start.12 = (bf16[256,768]{0,1:T(8,128)(2,1)S(1)}, bf16[256,768]{0,1:T(8,128)(2,1)}, u32[]{:S(2)}) copy-start(bf16[256,768]{0,1:T(8,128)(2,1)} %copy-done.11) | copy-start | bytes 1179652
  77.7 1.0 %copy-start.23 = (f32[6,256]{1,0:T(8,128)S(1)}, f32[6,256]{1,0:T(8,128)}, u32[]{:S(2)}) copy-start(f32[6,256]{1,0:T(8,128)} %copy-done.22) | copy-start | bytes 18436
  77.8 1.4 %copy-start.10 = (f32[6,256,256]{1,2,0:T(8,128)S(1)}, f32[6,256,256]{1,2,0:T(8,128)}, u32[]{:S(2)}) copy-start(f32[6,256,256]{1,2,0:T(8,128)} %copy-done.9) | copy-start | bytes 4718596
  79.6 1.0 %copy-start.2 = (bf16[1,1,256,768]{2,3,1,0:T(8,128)(2,1)S(1)}, bf16[1,1,256,768]{2,3,1,0:T(8,128)(2,1)}, u32[]{:S(2)}) copy-start(bf16[1,1,256,768]{2,3,1,0:T(8,128)(2,1)} %copy.160) | copy-start | bytes 1179652
  79.9 1.3 %copy-start.3 = (bf16[1,1,256,768]{2,3,1,0:T(8,128)(2,1)S(1)}, bf16[1,1,256,768]{2,3,1,0:T(8,128)(2,1)}, u32[]{:S(2)}) copy-start(bf16[1,1,256,768]{2,3,1,0:T(8,128)(2,1)} %copy.161) | copy-start | bytes 1179652
  81.5 0.9 %copy-start.15 = (f32[6,256]{0,1:T(8,128)S(1)}, f32[6,256]{0,1:T(8,128)}, u32[]{:S(2)}) copy-start(f32[6,256]{0,1:T(8,128)} %copy.119) | copy-start | bytes 18436
  81.7 1.1 %copy-start.5 = (bf16[1,256,768]{1,2,0:T(8,128)(2,1)S(1)}, bf16[1,256,768]{1,2,0:T(8,128)(2,1)}, u32[]{:S(2)}) copy-start(bf16[1,256,768]{1,2,0:T(8,128)(2,1)} %copy-done.4) | copy-start | bytes 1179652
  82.4 1.4 %copy-start.8 = (f32[6,256,256]{1,2,0:T(8,128)S(1)}, f32[6,256,256]{1,2,0:T(8,128)}, u32[]{:S(2)}) copy-start(f32[6,256,256]{1,2,0:T(8,128)} %copy-done.7) | copy-start | bytes 4718596
  84.5 1.0 %copy-start.1 = (bf16[1,1,256,768]{2,3,1,0:T(8,128)(2,1)S(1)}, bf16[1,1,256,768]{2,3,1,0:T(8,128)(2,1)}, u32[]{:S(2)}) copy-start(bf16[1,1,256,768]{2,3,1,0:T(8,128)(2,1)} %copy-done) | copy-start | bytes 1179652
where the time goes:
time: 88.1 us; the launch traced here: 87.2 us
  local copies, waits for them, and re-layouts  44.7 us (51%)
  starting transfers between devices  17.7 us (20%)
  waiting for transfers between devices  12.1 us (14%)
  other arithmetic  6.65 us (8%)
  matrix products  5.05 us (6%)
  between operations  1.09 us (1%)
    unnamed x63, local copies, waits for them, and re-layouts  30 us
    ppermute x2, waiting for transfers between devices, passed_along(): lax.ppermute(value, axis, [(source, source + steps) for source in range(l...  12.1 us
    ppermute x2, starting transfers between devices, passed_along(): lax.ppermute(value, axis, [(source, source + steps) for source in range(l...  7.17 us
    all_to_all x1, starting transfers between devices, local(): lax.all_to_all(stored_input[0], 'tensor', split_axis=2, concat_axis=1, ti...  5.29 us
    all_to_all x1, starting transfers between devices, local(): lax.all_to_all(block_scales[0], 'tensor', split_axis=2, concat_axis=1, ti...  5.2 us
    all_to_all x1, local copies, waits for them, and re-layouts, local(): lax.all_to_all(stored_input[0], 'tensor', split_axis=2, concat_axis=1, ti...  4.92 us
    another operation x4, local copies, waits for them, and re-layouts, to_heads(): return flat.reshape(tokens, width // HD, HD).transpose(1, 0, 2)  4.28 us
    sub x2, matrix products, attention_weights(): scores = scores - jnp.max(scores, axis=-1, keepdims=True)  2.21 us
  transfers between devices with their start and end apart: 4, of which 1 were waited for; matrix products, arithmetic and copies ran while one was open for 33% of the time, Pallas kernels for 0%

commit v1 on v0

v1 whole, which is shorter than its diff:
```python
import functools
import math

import jax
import jax.numpy as jnp
from jax import lax
from jax.experimental import pallas as pl
from jax.experimental.pallas import tpu as pltpu
from jax.sharding import PartitionSpec as P

HD = 128
SCALING = 1.0 / math.sqrt(HD)
EXP2_SCALE = SCALING * math.log2(math.e)
MESH = pl.DeviceIdType.MESH
STEPS = ((0, 1), (1, 1), (3, 1), (2, 1), (1, 0), (3, 0), (2, 0))


def across(a, b, dims):
    return lax.dot_general(a, b, (dims, ((), ())), preferred_element_type=jnp.float32)


def kernel(
    sections, heads,
    g_hbm, loss_hbm, q_hbm, k_hbm, x_hbm, s_hbm,
    next_hbm, qg_hbm, kg_hbm,
    xv, sv, gv, qv, kv, xs, xr, w, d0, d1, qo, ko,
    x_sem, s_sem, g_sem, q_sem, k_sem, own_sem, a2a_send, a2a_recv,
    r0_send, r1_send, r1_recv, qo_sem, ko_sem,
):
    section = lax.axis_index("section")
    me = lax.axis_index("tensor")
    x_me, y_me = me // 2, me % 2
    tokens = gv.shape[1]
    before = (section + sections - 1) % sections
    after = (section + 1) % sections
    is_last = section == sections - 1
    both = 2 * heads

    def partner(step, sign):
        dx, dy = step
        return ((x_me + 4 + sign * dx) % 4) * 2 + (y_me + dy) % 2

    def columns(h):
        return pl.ds(pl.multiple_of(h * HD, HD), HD)

    def q_copy(m, h):
        i = m * heads + h
        return pltpu.make_async_copy(q_hbm.at[0, m, :, columns(h)], qv.at[i], q_sem.at[i])

    def k_copy(m, h):
        i = m * heads + h
        return pltpu.make_async_copy(k_hbm.at[0, m, :, columns(h)], kv.at[i], k_sem.at[i])

    def g_copy(h):
        return pltpu.make_async_copy(g_hbm.at[0, :, columns(h)], gv.at[h], g_sem.at[h])

    def loss_copy(h):
        return pltpu.make_async_copy(
            loss_hbm.at[:, columns(h)], gv.at[heads + h], g_sem.at[heads + h]
        )

    def relay0(h):
        return pltpu.make_async_remote_copy(
            src_ref=d0.at[h], dst_ref=gv.at[heads + h],
            send_sem=r0_send.at[h], recv_sem=g_sem.at[heads + h],
            device_id={"section": before}, device_id_type=MESH,
        )

    def relay1(h):
        return pltpu.make_async_remote_copy(
            src_ref=d1.at[h], dst_ref=next_hbm.at[0, :, columns(h)],
            send_sem=r1_send.at[h], recv_sem=r1_recv.at[h],
            device_id={"section": before}, device_id_type=MESH,
        )

    def zero_copy(h):
        return pltpu.make_async_copy(
            qo.at[0], next_hbm.at[0, :, columns(h)], r1_recv.at[h]
        )

    def exchange(j):
        return pltpu.make_async_remote_copy(
            src_ref=xs.at[partner(STEPS[j], 1)], dst_ref=xr.at[me],
            send_sem=a2a_send.at[j], recv_sem=a2a_recv.at[j],
            device_id={"tensor": partner(STEPS[j], 1)}, device_id_type=MESH,
        )

    def arrival(j):
        return pltpu.make_async_remote_copy(
            src_ref=xs.at[me], dst_ref=xr.at[partner(STEPS[j], -1)],
            send_sem=a2a_send.at[j], recv_sem=a2a_recv.at[j],
            device_id={"tensor": partner(STEPS[j], 1)}, device_id_type=MESH,
        )

    def q_out(m, h):
        i = m * heads + h
        return pltpu.make_async_copy(qo.at[i], qg_hbm.at[0, m, :, columns(h)], qo_sem.at[i])

    def k_out(m, h):
        i = m * heads + h
        return pltpu.make_async_copy(ko.at[i], kg_hbm.at[0, m, :, columns(h)], ko_sem.at[i])

    barrier = pltpu.get_barrier_semaphore()
    for step in STEPS:
        pl.semaphore_signal(
            barrier, inc=1, device_id={"tensor": partner(step, 1)}, device_id_type=MESH
        )
    for other in (before, after):
        pl.semaphore_signal(
            barrier, inc=1, device_id={"section": other}, device_id_type=MESH
        )

    x_copy = pltpu.make_async_copy(x_hbm.at[0], xv, x_sem)
    s_copy = pltpu.make_async_copy(s_hbm.at[0], sv, s_sem)
    s_copy.start()
    x_copy.start()
    for h in range(heads):
        q_copy(0, h).start()
        k_copy(0, h).start()
        g_copy(h).start()
    for h in range(heads):
        q_copy(1, h).start()
        k_copy(1, h).start()

    @pl.when(is_last)
    def _():
        for h in range(heads):
            loss_copy(h).start()

    s_copy.wait()
    x_copy.wait()
    for m in range(2):
        scales = sv[m].astype(jnp.float32)
        for p in range(8):
            for h in range(heads):
                c = p * heads + h
                wide = xv[m, :, c * HD:(c + 1) * HD].astype(jnp.float32) * scales[:, c:c + 1]
                xs[p, m * heads + h] = wide.astype(jnp.bfloat16)

    pl.semaphore_wait(barrier, len(STEPS) + 2)
    for j in range(len(STEPS)):
        exchange(j).start()
    own_copy = pltpu.make_async_copy(xs.at[me], xr.at[me], own_sem)
    own_copy.start()

    causal = lax.broadcasted_iota(jnp.int32, (tokens, tokens), 1) >= lax.broadcasted_iota(
        jnp.int32, (tokens, tokens), 0
    )

    def weigh(i):
        scores = across(kv[i], qv[i], ((1,), (1,)))
        scores = jnp.where(causal, scores, -1e30)
        scores = scores - jnp.max(scores, axis=0, keepdims=True)
        expon = jnp.exp2(scores * EXP2_SCALE)
        weights = expon * (1.0 / jnp.sum(expon, axis=0, keepdims=True))
        w[i] = weights
        return weights

    def carry(weights, i):
        upstream = gv[i]
        carried = across(weights.astype(jnp.bfloat16), upstream, ((1,), (0,)))
        return (upstream.astype(jnp.float32) + carried).astype(jnp.bfloat16)

    def send_if(condition, copy):
        @pl.when(condition)
        def _():
            copy.start()

    @pl.loop(0, heads)
    def _(h):
        q_copy(0, h).wait()
        k_copy(0, h).wait()
        g_copy(h).wait()
        d0[h] = carry(weigh(h), h)
        send_if((h > 0) & (section > 0), relay0(jnp.maximum(h - 1, 0)))

    @pl.loop(0, heads)
    def _(h):
        q_copy(1, h).wait()
        k_copy(1, h).wait()
        weigh(heads + h)
        send_if((h == 0) & (section > 0), relay0(heads - 1))

    @pl.loop(0, heads)
    def _(h):
        relay0(h).wait_recv()
        d1[h] = carry(w[heads + h], heads + h)
        send_if((h > 0) & (section > 0), relay1(jnp.maximum(h - 1, 0)))

    own_copy.wait()
    for j in range(len(STEPS)):
        arrival(j).wait_recv()
    send_if(section > 0, relay1(heads - 1))

    @pl.loop(0, both)
    def _(i):
        weights, upstream = w[i], gv[i]
        inputs = xr[:, i].reshape(tokens, HD)
        product = across(inputs, upstream, ((1,), (1,)))
        centre = jnp.sum(weights * product, axis=0, keepdims=True)
        diff = (weights * (product - centre)).astype(jnp.bfloat16)
        ko[i] = (across(diff, qv[i], ((1,), (0,))) * SCALING).astype(jnp.bfloat16)
        qo[i] = (across(diff, kv[i], ((0,), (0,))) * SCALING).astype(jnp.bfloat16)

        @pl.when(i > 0)
        def _():
            n = jnp.maximum(i - 1, 0)
            q_out(n // heads, n % heads).start()
            k_out(n // heads, n % heads).start()

    @pl.when(section > 0)
    def _():
        for h in range(heads):
            relay0(h).wait_send()
            relay1(h).wait_send()

    q_out(1, heads - 1).start()
    k_out(1, heads - 1).start()
    for j in range(len(STEPS)):
        exchange(j).wait_send()
    for i in range(both):
        q_out(i // heads, i % heads).wait()
        k_out(i // heads, i % heads).wait()

    @pl.when(is_last)
    def _():
        qo[0] = jnp.zeros((tokens, HD), jnp.bfloat16)
        for h in range(heads):
            zero_copy(h).start()

    for h in range(heads):
        relay1(h).wait_recv()


def solution(mesh):
    sections = mesh.shape["section"]

    def local(grad_in, loss_grad, queries, attn_keys, stored_input, block_scales):
        tokens, width = loss_grad.shape
        heads = width // HD
        rows = stored_input.shape[2]
        both = 2 * heads
        parts = len(STEPS) + 1
        bf16, dma = jnp.bfloat16, pltpu.SemaphoreType.DMA
        anywhere = pl.BlockSpec(memory_space=pl.ANY)
        piece = (tokens, HD)
        return pl.pallas_call(
            functools.partial(kernel, sections, heads),
            out_shape=(
                jax.ShapeDtypeStruct(grad_in.shape, bf16),
                jax.ShapeDtypeStruct(queries.shape, bf16),
                jax.ShapeDtypeStruct(attn_keys.shape, bf16),
            ),
            in_specs=[anywhere] * 6,
            out_specs=(anywhere,) * 3,
            scratch_shapes=[
                pltpu.VMEM(stored_input.shape[1:], bf16),
                pltpu.VMEM(block_scales.shape[1:], bf16),
                pltpu.VMEM((both, *piece), bf16),
                pltpu.VMEM((both, *piece), bf16),
                pltpu.VMEM((both, *piece), bf16),
                pltpu.VMEM((parts, both, rows, HD), bf16),
                pltpu.VMEM((parts, both, rows, HD), bf16),
                pltpu.VMEM((both, tokens, tokens), jnp.float32),
                pltpu.VMEM((heads, *piece), bf16),
                pltpu.VMEM((heads, *piece), bf16),
                pltpu.VMEM((both, *piece), bf16),
                pltpu.VMEM((both, *piece), bf16),
                dma, dma, dma((both,)), dma((both,)), dma((both,)), dma,
                dma((len(STEPS),)), dma((len(STEPS),)),
                dma((heads,)), dma((heads,)), dma((heads,)),
                dma((both,)), dma((both,)),
            ],
            compiler_params=pltpu.CompilerParams(collective_id=0, has_side_effects=True),
            name="relay_attention",
        )(grad_in, loss_grad, queries, attn_keys, stored_input, block_scales)

    return jax.shard_map(
        local,
        mesh=mesh,
        in_specs=(
            P("section", None, "tensor"),
            P(None, "tensor"),
            P("section", None, None, "tensor"),
            P("section", None, None, "tensor"),
            P("section", None, "tensor", None),
            P("section", None, "tensor", None),
        ),
        out_specs=(
            P("section", None, "tensor"),
            P("section", None, None, "tensor"),
            P("section", None, None, "tensor"),
        ),
        check_vma=False,
    )
```

time: 88.1 us -> 41.7 us (0.47)
  the two profiles are of different devices: /device:TPU:249 before, /device:TPU:25 now
where the time goes in v1:
time: 41.7 us; the launch traced here: 41.5 us
  Pallas kernels  36.7 us (88%)
  local copies, waits for them, and re-layouts  4.14 us (10%)
  between operations  0.65 us (2%)
    pallas_call x1, Pallas kernels, local(): pl.pallas_call(functools.partial(kernel, sections, heads), out_shape=(jax...  36.7 us
    unnamed x7, local copies, waits for them, and re-layouts  4.14 us

profile of v1, /device:TPU:25, one launch (start us, length us, event | category | flops | bytes accessed | tf_op | source)
XLA Modules:
  0.0 41.5 jit_solution(9045390370437368243)
XLA Ops:
  0.6 36.7 %relay_attention.1 = (bf16[1,256,768]{2,1,0:T(8,128)(2,1)}, bf16[1,2,256,768]{3,2,1,0:T(8,128)(2,1)}, bf16[1,2,256,768]{3,2,1,0:T(8,128)(2,1)}) custom-call(bf16[1,256,768]{2,1,0:T(8,128)(2,1)} %g_hbm.1, bf16[256,768]{1,0:T(8,128)(2,1)} %loss_hbm.1, bf16[1,2,256,768]{3,2,1,0:T(8,128)(2,1)} %q_hbm.1, bf16[1,2,256,768]{3,2,1,0:T(8,128)(2,1)} %k_hbm.1, ...), custom_call_target="tpu_custom_call" | custom-call | tf_op jit(solution)/shard_map/relay_attention/pallas_call | solution.py:247
  37.3 0.0 copy-start.1
  37.3 1.8 %copy.12 = bf16[1,256,768]{2,1,0:T(8,128)(2,1)} copy(bf16[1,256,768]{2,1,0:T(8,128)(2,1)} %get-tuple-element.6) | data formatting | bytes 786432
  39.2 0.0 copy-done.1
  39.2 0.0 copy-start
  39.2 0.9 %copy.13 = bf16[1,2,256,768]{3,2,1,0:T(8,128)(2,1)} copy(bf16[1,2,256,768]{3,2,1,0:T(8,128)(2,1)S(1)} %copy-done.1) | data formatting | bytes 1572864
  40.1 0.5 %copy-done = bf16[1,2,256,768]{3,2,1,0:T(8,128)(2,1)S(1)} copy-done((bf16[1,2,256,768]{3,2,1,0:T(8,128)(2,1)S(1)}, bf16[1,2,256,768]{3,2,1,0:T(8,128)(2,1)}, u32[]{:S(2)}) %copy-start) | copy-done | bytes 786456
  40.6 0.9 %copy.14 = bf16[1,2,256,768]{3,2,1,0:T(8,128)(2,1)} copy(bf16[1,2,256,768]{3,2,1,0:T(8,128)(2,1)S(1)} %copy-done) | data formatting | bytes 1572864
Async XLA Ops:
  37.3 1.9 %copy-start.1 = (bf16[1,2,256,768]{3,2,1,0:T(8,128)(2,1)S(1)}, bf16[1,2,256,768]{3,2,1,0:T(8,128)(2,1)}, u32[]{:S(2)}) copy-start(bf16[1,2,256,768]{3,2,1,0:T(8,128)(2,1)} %get-tuple-element.7) | copy-start | bytes 2359300
  39.2 1.4 %copy-start = (bf16[1,2,256,768]{3,2,1,0:T(8,128)(2,1)S(1)}, bf16[1,2,256,768]{3,2,1,0:T(8,128)(2,1)}, u32[]{:S(2)}) copy-start(bf16[1,2,256,768]{3,2,1,0:T(8,128)(2,1)} %get-tuple-element.8) | copy-start | bytes 2359300

commit v2 on v1

--- a/solution.py
+++ b/solution.py
@@ -22,10 +22,10 @@
 def kernel(
     sections, heads,
     g_hbm, loss_hbm, q_hbm, k_hbm, x_hbm, s_hbm,
-    next_hbm, qg_hbm, kg_hbm,
-    xv, sv, gv, qv, kv, xs, xr, w, d0, d1, qo, ko,
+    landed, qo, ko,
+    xv, sv, gv, qv, kv, xs, xr, w, d0, d1,
     x_sem, s_sem, g_sem, q_sem, k_sem, own_sem, a2a_send, a2a_recv,
-    r0_send, r1_send, r1_recv, qo_sem, ko_sem,
+    r0_send, r1_send, r1_recv,
 ):
     section = lax.axis_index("section")
     me = lax.axis_index("tensor")
@@ -68,14 +68,9 @@
 
     def relay1(h):
         return pltpu.make_async_remote_copy(
-            src_ref=d1.at[h], dst_ref=next_hbm.at[0, :, columns(h)],
+            src_ref=d1.at[h], dst_ref=landed.at[h],
             send_sem=r1_send.at[h], recv_sem=r1_recv.at[h],
             device_id={"section": before}, device_id_type=MESH,
-        )
-
-    def zero_copy(h):
-        return pltpu.make_async_copy(
-            qo.at[0], next_hbm.at[0, :, columns(h)], r1_recv.at[h]
         )
 
     def exchange(j):
@@ -91,14 +86,6 @@
             send_sem=a2a_send.at[j], recv_sem=a2a_recv.at[j],
             device_id={"tensor": partner(STEPS[j], 1)}, device_id_type=MESH,
         )
-
-    def q_out(m, h):
-        i = m * heads + h
-        return pltpu.make_async_copy(qo.at[i], qg_hbm.at[0, m, :, columns(h)], qo_sem.at[i])
-
-    def k_out(m, h):
-        i = m * heads + h
-        return pltpu.make_async_copy(ko.at[i], kg_hbm.at[0, m, :, columns(h)], ko_sem.at[i])
 
     barrier = pltpu.get_barrier_semaphore()
     for step in STEPS:
@@ -202,57 +189,65 @@
         ko[i] = (across(diff, qv[i], ((1,), (0,))) * SCALING).astype(jnp.bfloat16)
         qo[i] = (across(diff, kv[i], ((0,), (0,))) * SCALING).astype(jnp.bfloat16)
 
-        @pl.when(i > 0)
-        def _():
-            n = jnp.maximum(i - 1, 0)
-            q_out(n // heads, n % heads).start()
-            k_out(n // heads, n % heads).start()
-
     @pl.when(section > 0)
     def _():
         for h in range(heads):
             relay0(h).wait_send()
             relay1(h).wait_send()
 
-    q_out(1, heads - 1).start()
-    k_out(1, heads - 1).start()
     for j in range(len(STEPS)):
         exchange(j).wait_send()
-    for i in range(both):
-        q_out(i // heads, i % heads).wait()
-        k_out(i // heads, i % heads).wait()
+
+    @pl.when(jnp.logical_not(is_last))
+    def _():
+        for h in range(heads):
+            relay1(h).wait_recv()
 
     @pl.when(is_last)
     def _():
-        qo[0] = jnp.zeros((tokens, HD), jnp.bfloat16)
-        for h in range(heads):
-            zero_copy(h).start()
-
-    for h in range(heads):
-        relay1(h).wait_recv()
+        landed[...] = jnp.zeros_like(landed)
+
+
+def place(heads, landed, qo, ko, next_hbm, qg_hbm, kg_hbm, next_sem, q_sem, k_sem):
+    copies = []
+    for i in range(2 * heads):
+        m, h = divmod(i, heads)
+        cols = pl.ds(h * HD, HD)
+        copies.append(pltpu.make_async_copy(qo.at[i], qg_hbm.at[0, m, :, cols], q_sem.at[i]))
+        copies.append(pltpu.make_async_copy(ko.at[i], kg_hbm.at[0, m, :, cols], k_sem.at[i]))
+        if m == 0:
+            copies.append(
+                pltpu.make_async_copy(landed.at[h], next_hbm.at[0, :, cols], next_sem.at[h])
+            )
+    for copy in copies:
+        copy.start()
+    for copy in copies:
+        copy.wait()
 
 
 def solution(mesh):
     sections = mesh.shape["section"]
 
-    def local(grad_in, loss_grad, queries, attn_keys, stored_input, block_scales):
+    def local(*arguments):
+        grad_in, loss_grad, queries, attn_keys, stored_input, block_scales = arguments
         tokens, width = loss_grad.shape
         heads = width // HD
         rows = stored_input.shape[2]
         both = 2 * heads
         parts = len(STEPS) + 1
         bf16, dma = jnp.bfloat16, pltpu.SemaphoreType.DMA
-        anywhere = pl.BlockSpec(memory_space=pl.ANY)
+        anywhere = pl.BlockSpec(memory_space=pltpu.HBM)
         piece = (tokens, HD)
-        return pl.pallas_call(
+        inside = pl.BlockSpec(memory_space=pltpu.VMEM)
+        held = pl.pallas_call(
             functools.partial(kernel, sections, heads),
             out_shape=(
-                jax.ShapeDtypeStruct(grad_in.shape, bf16),
-                jax.ShapeDtypeStruct(queries.shape, bf16),
-                jax.ShapeDtypeStruct(attn_keys.shape, bf16),
+                jax.ShapeDtypeStruct((heads, *piece), bf16),
+                jax.ShapeDtypeStruct((both, *piece), bf16),
+                jax.ShapeDtypeStruct((both, *piece), bf16),
             ),
             in_specs=[anywhere] * 6,
-            out_specs=(anywhere,) * 3,
+            out_specs=(inside,) * 3,
             scratch_shapes=[
                 pltpu.VMEM(stored_input.shape[1:], bf16),
                 pltpu.VMEM(block_scales.shape[1:], bf16),
@@ -264,16 +259,28 @@
                 pltpu.VMEM((both, tokens, tokens), jnp.float32),
                 pltpu.VMEM((heads, *piece), bf16),
                 pltpu.VMEM((heads, *piece), bf16),
-                pltpu.VMEM((both, *piece), bf16),
-                pltpu.VMEM((both, *piece), bf16),
                 dma, dma, dma((both,)), dma((both,)), dma((both,)), dma,
                 dma((len(STEPS),)), dma((len(STEPS),)),
                 dma((heads,)), dma((heads,)), dma((heads,)),
-                dma((both,)), dma((both,)),
             ],
-            compiler_params=pltpu.CompilerParams(collective_id=0, has_side_effects=True),
+            compiler_params=pltpu.CompilerParams(
+                collective_id=0, has_side_effects=True, vmem_limit_bytes=24 * 2**20
+            ),
             name="relay_attention",
-        )(grad_in, loss_grad, queries, attn_keys, stored_input, block_scales)
+        )(*(pltpu.with_memory_space_constraint(a, pltpu.HBM) for a in arguments))
+        return pl.pallas_call(
+            functools.partial(place, heads),
+            out_shape=(
+                jax.ShapeDtypeStruct(grad_in.shape, bf16),
+                jax.ShapeDtypeStruct(queries.shape, bf16),
+                jax.ShapeDtypeStruct(attn_keys.shape, bf16),
+            ),
+            in_specs=[inside] * 3,
+            out_specs=(anywhere,) * 3,
+            scratch_shapes=[dma((heads,)), dma((both,)), dma((both,))],
+            compiler_params=pltpu.CompilerParams(vmem_limit_bytes=8 * 2**20),
+            name="place",
+        )(*held)
 
     return jax.shard_map(
         local,

time: 41.7 us -> 38.1 us (0.914)
  local copies, waits for them, and re-layouts: 4.14 us -> 0 us
  Pallas kernels: 36.7 us -> 37.3 us
    unnamed x7 -> x0, local copies, waits for them, and re-layouts: 4.14 us -> none
    pallas_call x0 -> x1, Pallas kernels: none -> 1.51 us  [local(): pl.pallas_call(functools.partial(place, heads), out_shape=(jax.ShapeDtype...]
    pallas_call x1, Pallas kernels: 36.7 us -> 35.8 us  [local(): pl.pallas_call(functools.partial(kernel, sections, heads), out_shape=(jax...]
where the time goes in v2:
time: 38.1 us; the launch traced here: 37.9 us
  Pallas kernels  37.3 us (98%)
  between operations  0.64 us (2%)
    pallas_call x1, Pallas kernels, local(): pl.pallas_call(functools.partial(kernel, sections, heads), out_shape=(jax...  35.8 us
    pallas_call x1, Pallas kernels, local(): pl.pallas_call(functools.partial(place, heads), out_shape=(jax.ShapeDtype...  1.51 us

profile of v2, /device:TPU:25, one launch (start us, length us, event | category | flops | bytes accessed | tf_op | source)
XLA Modules:
  0.0 37.9 jit_solution(358699932549223381)
XLA Ops:
  0.6 35.8 %relay_attention.1 = (bf16[6,256,128]{2,1,0:T(8,128)(2,1)S(1)}, bf16[12,256,128]{2,1,0:T(8,128)(2,1)S(1)}, bf16[12,256,128]{2,1,0:T(8,128)(2,1)S(1)}) custom-call(bf16[1,256,768]{2,1,0:T(8,128)(2,1)} %g_hbm.1, bf16[256,768]{1,0:T(8,128)(2,1)} %loss_hbm.1, bf16[1,2,256,768]{3,2,1,0:T(8,128)(2,1)} %q_hbm.1, bf16[1,2,256,768]{3,2,1,0:T(8,128)(2,1)} %k_hbm.1, ...), custom_call_target="tpu_custom_call" | custom-call | tf_op jit(solution)/shard_map/relay_attention/pallas_call | solution.py:242
  36.4 1.5 %place.1 = (bf16[1,256,768]{2,1,0:T(8,128)(2,1)}, bf16[1,2,256,768]{3,2,1,0:T(8,128)(2,1)}, bf16[1,2,256,768]{3,2,1,0:T(8,128)(2,1)}) custom-call(bf16[6,256,128]{2,1,0:T(8,128)(2,1)S(1)} %get-tuple-element.6.landed, bf16[12,256,128]{2,1,0:T(8,128)(2,1)S(1)} %get-tuple-element.7.qo, bf16[12,256,128]{2,1,0:T(8,128)(2,1)S(1)} %get-tuple-element.8.ko), custom_call_target="tpu_custom_call" | custom-call | tf_op jit(solution)/shard_map/place/pallas_call | solution.py:271

commit v3 on v2

--- a/solution.py
+++ b/solution.py
@@ -11,6 +11,7 @@
 HD = 128
 SCALING = 1.0 / math.sqrt(HD)
 EXP2_SCALE = SCALING * math.log2(math.e)
+PAIR = 2
 MESH = pl.DeviceIdType.MESH
 STEPS = ((0, 1), (1, 1), (3, 1), (2, 1), (1, 0), (3, 0), (2, 0))
 
@@ -134,60 +135,80 @@
         jnp.int32, (tokens, tokens), 0
     )
 
-    def weigh(i):
-        scores = across(kv[i], qv[i], ((1,), (1,)))
+    def weigh(keys, queries):
+        scores = across(keys, queries, ((1,), (1,)))
         scores = jnp.where(causal, scores, -1e30)
         scores = scores - jnp.max(scores, axis=0, keepdims=True)
         expon = jnp.exp2(scores * EXP2_SCALE)
-        weights = expon * (1.0 / jnp.sum(expon, axis=0, keepdims=True))
-        w[i] = weights
-        return weights
-
-    def carry(weights, i):
-        upstream = gv[i]
+        return expon * (1.0 / jnp.sum(expon, axis=0, keepdims=True))
+
+    def carry(weights, upstream):
         carried = across(weights.astype(jnp.bfloat16), upstream, ((1,), (0,)))
         return (upstream.astype(jnp.float32) + carried).astype(jnp.bfloat16)
 
-    def send_if(condition, copy):
+    def score_grads(weights, upstream, inputs, queries, keys):
+        product = across(inputs, upstream, ((1,), (1,)))
+        centre = jnp.sum(weights * product, axis=0, keepdims=True)
+        diff = (weights * (product - centre)).astype(jnp.bfloat16)
+        for_keys = across(diff, queries, ((1,), (0,))) * SCALING
+        for_queries = across(diff, keys, ((0,), (0,))) * SCALING
+        return for_queries.astype(jnp.bfloat16), for_keys.astype(jnp.bfloat16)
+
+    def send_if(condition, relay, n):
         @pl.when(condition)
         def _():
-            copy.start()
-
-    @pl.loop(0, heads)
-    def _(h):
-        q_copy(0, h).wait()
-        k_copy(0, h).wait()
-        g_copy(h).wait()
-        d0[h] = carry(weigh(h), h)
-        send_if((h > 0) & (section > 0), relay0(jnp.maximum(h - 1, 0)))
-
-    @pl.loop(0, heads)
-    def _(h):
-        q_copy(1, h).wait()
-        k_copy(1, h).wait()
-        weigh(heads + h)
-        send_if((h == 0) & (section > 0), relay0(heads - 1))
-
-    @pl.loop(0, heads)
-    def _(h):
-        relay0(h).wait_recv()
-        d1[h] = carry(w[heads + h], heads + h)
-        send_if((h > 0) & (section > 0), relay1(jnp.maximum(h - 1, 0)))
+            for h in range(PAIR):
+                relay(n * PAIR + h).start()
+
+    def group(n):
+        return [n * PAIR + h for h in range(PAIR)]
+
+    steps = heads // PAIR
+
+    @pl.loop(0, steps)
+    def _(n):
+        for h in group(n):
+            q_copy(0, h).wait()
+            k_copy(0, h).wait()
+            g_copy(h).wait()
+            q_copy(1, h).wait()
+            k_copy(1, h).wait()
+        here = group(n) + [heads + h for h in group(n)]
+        loaded = [(kv[i], qv[i]) for i in here]
+        upstream = [gv[h] for h in group(n)]
+        weights = [weigh(*pair) for pair in loaded]
+        carried = [carry(*pair) for pair in zip(weights, upstream)]
+        for h, value in zip(group(n), carried):
+            d0[h] = value
+        for i, value in zip(here, weights):
+            w[i] = value
+        send_if((n > 0) & (section > 0), relay0, jnp.maximum(n - 1, 0))
+
+    @pl.loop(0, steps)
+    def _(n):
+        send_if((n == 0) & (section > 0), relay0, steps - 1)
+        for h in group(n):
+            relay0(h).wait_recv()
+        loaded = [(w[heads + h], gv[heads + h]) for h in group(n)]
+        carried = [carry(*pair) for pair in loaded]
+        for h, value in zip(group(n), carried):
+            d1[h] = value
+        send_if((n > 0) & (section > 0), relay1, jnp.maximum(n - 1, 0))
 
     own_copy.wait()
     for j in range(len(STEPS)):
         arrival(j).wait_recv()
-    send_if(section > 0, relay1(heads - 1))
-
-    @pl.loop(0, both)
-    def _(i):
-        weights, upstream = w[i], gv[i]
-        inputs = xr[:, i].reshape(tokens, HD)
-        product = across(inputs, upstream, ((1,), (1,)))
-        centre = jnp.sum(weights * product, axis=0, keepdims=True)
-        diff = (weights * (product - centre)).astype(jnp.bfloat16)
-        ko[i] = (across(diff, qv[i], ((1,), (0,))) * SCALING).astype(jnp.bfloat16)
-        qo[i] = (across(diff, kv[i], ((0,), (0,))) * SCALING).astype(jnp.bfloat16)
+    send_if(section > 0, relay1, steps - 1)
+
+    @pl.loop(0, 2 * steps)
+    def _(n):
+        loaded = [
+            (w[i], gv[i], xr[:, i].reshape(tokens, HD), qv[i], kv[i]) for i in group(n)
+        ]
+        results = [score_grads(*values) for values in loaded]
+        for i, (for_queries, for_keys) in zip(group(n), results):
+            qo[i] = for_queries
+            ko[i] = for_keys
 
     @pl.when(section > 0)
     def _():

time: 38.1 us -> 38.3 us (level)
  the two profiles are of different devices: /device:TPU:25 before, /device:TPU:17 now
where the time goes in v3:
time: 38.3 us; the launch traced here: 38.2 us
  Pallas kernels  37.5 us (98%)
  between operations  0.64 us (2%)
    pallas_call x1, Pallas kernels, local(): pl.pallas_call(functools.partial(kernel, sections, heads), out_shape=(jax...  36 us
    pallas_call x1, Pallas kernels, local(): pl.pallas_call(functools.partial(place, heads), out_shape=(jax.ShapeDtype...  1.51 us

profile of v3, /device:TPU:17, one launch (start us, length us, event | category | flops | bytes accessed | tf_op | source)
XLA Modules:
  0.0 38.2 jit_solution(10233810478662980729)
XLA Ops:
  0.6 36.0 %relay_attention.1 = (bf16[6,256,128]{2,1,0:T(8,128)(2,1)S(1)}, bf16[12,256,128]{2,1,0:T(8,128)(2,1)S(1)}, bf16[12,256,128]{2,1,0:T(8,128)(2,1)S(1)}) custom-call(bf16[1,256,768]{2,1,0:T(8,128)(2,1)} %g_hbm.1, bf16[256,768]{1,0:T(8,128)(2,1)} %loss_hbm.1, bf16[1,2,256,768]{3,2,1,0:T(8,128)(2,1)} %q_hbm.1, bf16[1,2,256,768]{3,2,1,0:T(8,128)(2,1)} %k_hbm.1, ...), custom_call_target="tpu_custom_call" | custom-call | tf_op jit(solution)/shard_map/relay_attention/pallas_call | solution.py:263
  36.7 1.5 %place.1 = (bf16[1,256,768]{2,1,0:T(8,128)(2,1)}, bf16[1,2,256,768]{3,2,1,0:T(8,128)(2,1)}, bf16[1,2,256,768]{3,2,1,0:T(8,128)(2,1)}) custom-call(bf16[6,256,128]{2,1,0:T(8,128)(2,1)S(1)} %get-tuple-element.6.landed, bf16[12,256,128]{2,1,0:T(8,128)(2,1)S(1)} %get-tuple-element.7.qo, bf16[12,256,128]{2,1,0:T(8,128)(2,1)S(1)} %get-tuple-element.8.ko), custom_call_target="tpu_custom_call" | custom-call | tf_op jit(solution)/shard_map/place/pallas_call | solution.py:292

commit v4 on v3

--- a/solution.py
+++ b/solution.py
@@ -153,12 +153,6 @@
         for_keys = across(diff, queries, ((1,), (0,))) * SCALING
         for_queries = across(diff, keys, ((0,), (0,))) * SCALING
         return for_queries.astype(jnp.bfloat16), for_keys.astype(jnp.bfloat16)
-
-    def send_if(condition, relay, n):
-        @pl.when(condition)
-        def _():
-            for h in range(PAIR):
-                relay(n * PAIR + h).start()
 
     def group(n):
         return [n * PAIR + h for h in range(PAIR)]
@@ -182,23 +176,23 @@
             d0[h] = value
         for i, value in zip(here, weights):
             w[i] = value
-        send_if((n > 0) & (section > 0), relay0, jnp.maximum(n - 1, 0))
-
-    @pl.loop(0, steps)
-    def _(n):
-        send_if((n == 0) & (section > 0), relay0, steps - 1)
-        for h in group(n):
-            relay0(h).wait_recv()
-        loaded = [(w[heads + h], gv[heads + h]) for h in group(n)]
-        carried = [carry(*pair) for pair in loaded]
-        for h, value in zip(group(n), carried):
-            d1[h] = value
-        send_if((n > 0) & (section > 0), relay1, jnp.maximum(n - 1, 0))
+        @pl.when(section > 0)
+        def _():
+            for h in group(n):
+                relay0(h).start()
+
+    @pl.loop(0, heads)
+    def _(h):
+        relay0(h).wait_recv()
+        d1[h] = carry(w[heads + h], gv[heads + h])
+
+        @pl.when(section > 0)
+        def _():
+            relay1(h).start()
 
     own_copy.wait()
     for j in range(len(STEPS)):
         arrival(j).wait_recv()
-    send_if(section > 0, relay1, steps - 1)
 
     @pl.loop(0, 2 * steps)
     def _(n):

time: 38.3 us -> 36.4 us (0.950)
  the two profiles are of different devices: /device:TPU:17 before, /device:TPU:255 now
where the time goes in v4:
time: 36.4 us; the launch traced here: 36.2 us
  Pallas kernels  35.6 us (98%)
  between operations  0.64 us (2%)
    pallas_call x1, Pallas kernels, local(): pl.pallas_call(functools.partial(kernel, sections, heads), out_shape=(jax...  34 us
    pallas_call x1, Pallas kernels, local(): pl.pallas_call(functools.partial(place, heads), out_shape=(jax.ShapeDtype...  1.51 us

profile of v4, /device:TPU:255, one launch (start us, length us, event | category | flops | bytes accessed | tf_op | source)
XLA Modules:
  0.0 36.2 jit_solution(18016707112709669121)
XLA Ops:
  0.6 34.0 %relay_attention.1 = (bf16[6,256,128]{2,1,0:T(8,128)(2,1)S(1)}, bf16[12,256,128]{2,1,0:T(8,128)(2,1)S(1)}, bf16[12,256,128]{2,1,0:T(8,128)(2,1)S(1)}) custom-call(bf16[1,256,768]{2,1,0:T(8,128)(2,1)} %g_hbm.1, bf16[256,768]{1,0:T(8,128)(2,1)} %loss_hbm.1, bf16[1,2,256,768]{3,2,1,0:T(8,128)(2,1)} %q_hbm.1, bf16[1,2,256,768]{3,2,1,0:T(8,128)(2,1)} %k_hbm.1, ...), custom_call_target="tpu_custom_call" | custom-call | tf_op jit(solution)/shard_map/relay_attention/pallas_call | solution.py:257
  34.7 1.5 %place.1 = (bf16[1,256,768]{2,1,0:T(8,128)(2,1)}, bf16[1,2,256,768]{3,2,1,0:T(8,128)(2,1)}, bf16[1,2,256,768]{3,2,1,0:T(8,128)(2,1)}) custom-call(bf16[6,256,128]{2,1,0:T(8,128)(2,1)S(1)} %get-tuple-element.6.landed, bf16[12,256,128]{2,1,0:T(8,128)(2,1)S(1)} %get-tuple-element.7.qo, bf16[12,256,128]{2,1,0:T(8,128)(2,1)S(1)} %get-tuple-element.8.ko), custom_call_target="tpu_custom_call" | custom-call | tf_op jit(solution)/shard_map/place/pallas_call | solution.py:286

commit v5 on v4

--- a/solution.py
+++ b/solution.py
@@ -201,8 +201,8 @@
         ]
         results = [score_grads(*values) for values in loaded]
         for i, (for_queries, for_keys) in zip(group(n), results):
-            qo[i] = for_queries
-            ko[i] = for_keys
+            qo[n // steps, :, columns(i % heads)] = for_queries
+            ko[n // steps, :, columns(i % heads)] = for_keys
 
     @pl.when(section > 0)
     def _():
@@ -225,15 +225,15 @@
 
 def place(heads, landed, qo, ko, next_hbm, qg_hbm, kg_hbm, next_sem, q_sem, k_sem):
     copies = []
-    for i in range(2 * heads):
-        m, h = divmod(i, heads)
-        cols = pl.ds(h * HD, HD)
-        copies.append(pltpu.make_async_copy(qo.at[i], qg_hbm.at[0, m, :, cols], q_sem.at[i]))
-        copies.append(pltpu.make_async_copy(ko.at[i], kg_hbm.at[0, m, :, cols], k_sem.at[i]))
-        if m == 0:
-            copies.append(
-                pltpu.make_async_copy(landed.at[h], next_hbm.at[0, :, cols], next_sem.at[h])
+    for m in range(2):
+        copies.append(pltpu.make_async_copy(qo.at[m], qg_hbm.at[0, m], q_sem.at[m]))
+        copies.append(pltpu.make_async_copy(ko.at[m], kg_hbm.at[0, m], k_sem.at[m]))
+    for h in range(heads):
+        copies.append(
+            pltpu.make_async_copy(
+                landed.at[h], next_hbm.at[0, :, pl.ds(h * HD, HD)], next_sem.at[h]
             )
+        )
     for copy in copies:
         copy.start()
     for copy in copies:
@@ -258,8 +258,8 @@
             functools.partial(kernel, sections, heads),
             out_shape=(
                 jax.ShapeDtypeStruct((heads, *piece), bf16),
-                jax.ShapeDtypeStruct((both, *piece), bf16),
-                jax.ShapeDtypeStruct((both, *piece), bf16),
+                jax.ShapeDtypeStruct(queries.shape[1:], bf16),
+                jax.ShapeDtypeStruct(attn_keys.shape[1:], bf16),
             ),
             in_specs=[anywhere] * 6,
             out_specs=(inside,) * 3,
@@ -292,7 +292,7 @@
             ),
             in_specs=[inside] * 3,
             out_specs=(anywhere,) * 3,
-            scratch_shapes=[dma((heads,)), dma((both,)), dma((both,))],
+            scratch_shapes=[dma((heads,)), dma((2,)), dma((2,))],
             compiler_params=pltpu.CompilerParams(vmem_limit_bytes=8 * 2**20),
             name="place",
         )(*held)

time: 36.4 us -> 36.2 us (level)
  no operation moved by 1% of the time
where the time goes in v5:
time: 36.2 us; the launch traced here: 36 us
  Pallas kernels  35.4 us (98%)
  between operations  0.64 us (2%)
    pallas_call x1, Pallas kernels, local(): pl.pallas_call(functools.partial(kernel, sections, heads), out_shape=(jax...  34 us
    pallas_call x1, Pallas kernels, local(): pl.pallas_call(functools.partial(place, heads), out_shape=(jax.ShapeDtype...  1.34 us

profile of v5, /device:TPU:255, one launch (start us, length us, event | category | flops | bytes accessed | tf_op | source)
XLA Modules:
  0.0 36.0 jit_solution(7027068269660436551)
XLA Ops:
  0.6 34.0 %relay_attention.1 = (bf16[6,256,128]{2,1,0:T(8,128)(2,1)S(1)}, bf16[2,256,768]{2,1,0:T(8,128)(2,1)S(1)}, bf16[2,256,768]{2,1,0:T(8,128)(2,1)S(1)}) custom-call(bf16[1,256,768]{2,1,0:T(8,128)(2,1)} %g_hbm.1, bf16[256,768]{1,0:T(8,128)(2,1)} %loss_hbm.1, bf16[1,2,256,768]{3,2,1,0:T(8,128)(2,1)} %q_hbm.1, bf16[1,2,256,768]{3,2,1,0:T(8,128)(2,1)} %k_hbm.1, ...), custom_call_target="tpu_custom_call" | custom-call | tf_op jit(solution)/shard_map/relay_attention/pallas_call | solution.py:257
  34.7 1.3 %place.1 = (bf16[1,256,768]{2,1,0:T(8,128)(2,1)}, bf16[1,2,256,768]{3,2,1,0:T(8,128)(2,1)}, bf16[1,2,256,768]{3,2,1,0:T(8,128)(2,1)}) custom-call(bf16[6,256,128]{2,1,0:T(8,128)(2,1)S(1)} %get-tuple-element.6.landed, bf16[2,256,768]{2,1,0:T(8,128)(2,1)S(1)} %get-tuple-element.7.qo, bf16[2,256,768]{2,1,0:T(8,128)(2,1)S(1)} %get-tuple-element.8.ko), custom_call_target="tpu_custom_call" | custom-call | tf_op jit(solution)/shard_map/place/pallas_call | solution.py:286
